TPU v7x, 128 devices: a whole 4x4x4 slice. The times are simulated.
128 devices in a mesh: ctx: 16 (over x_lo, z, core), head: 8 (over x_hi, y).
Axes of the slice: x: 4 (x_hi: 2, x_lo: 2; x = x_hi * 2 + x_lo), y: 4, z: 4, core: 2. Of those that a mesh axis runs over, the one named last changes fastest.
Arguments:
- queries: bfloat16 [4096, 4096], P(('ctx', 'head')), may hold values from -10 to 10
- keys: bfloat16 [4096, 4096], P(('ctx', 'head')), may hold values from -10 to 10
- values: bfloat16 [4096, 4096], P(('ctx', 'head')), may hold values from -6 to 6
- grad_out: bfloat16 [4096, 4096], P(('ctx', 'head')), may hold values from -6 to 6
- block_doc: int32 [32], replicated, may hold values from 0 to 7, as said below
Outputs:
- attn_out: bfloat16 [4096, 4096], P(('ctx', 'head'))
- d_q: bfloat16 [4096, 4096], P(('ctx', 'head'))
- d_k: bfloat16 [4096, 4096], P(('ctx', 'head'))
- d_v: bfloat16 [4096, 4096], P(('ctx', 'head'))
Inputs may be any that keep to these rules, and one draw needn't show every extreme that they name: `block_doc`: document numbers never fall; every document covers at least one block; the last document covers exactly 16 blocks and every other one fewer.
All inputs are finite; a program needn't handle non-finite values.
Results may differ from a plain program's by a relative error of at most 0.03.
Values may be sent and summed in bfloat16 or wider, within the bound.
No kernel may reach another device: no remote copies, remote signals or barrier semaphores. Data moves between devices by JAX's collectives and lax.ppermute only.
A program may use at most 128 MiB of HBM per device.

v0:
```python
import math
import jax
import jax.numpy as jnp
from jax import lax
from jax.sharding import PartitionSpec as P

HD = 128
BLK = 128
masked_low = -1e30


def document_of(block_doc, positions):
    hits = positions[:, None] // BLK == lax.iota(jnp.int32, block_doc.shape[0])[None, :]
    return jnp.sum(jnp.where(hits, block_doc[None, :], 0), axis=1)


def token_positions(first_row, count, row_count, cycle_size):
    rows = first_row + lax.iota(jnp.int32, count)
    owner = rows // row_count
    local = rows % row_count
    half = row_count // 2
    return jnp.where(
        local < half, owner * half + local, (2 * cycle_size - 1 - owner) * half + local - half
    )


def visible(block_doc, query_pos, key_pos):
    same_doc = (
        document_of(block_doc, query_pos)[:, None] == document_of(block_doc, key_pos)[None, :]
    )
    return same_doc & (key_pos[None, :] <= query_pos[:, None])


def forward_update(running, query_heads, key_part, value_part, live, score_scale):
    accum, run_max, run_sum = running
    scores = (
        jnp.einsum("qhd,khd->hqk", query_heads, key_part, preferred_element_type=jnp.float32)
        * score_scale
    )
    scores = jnp.where(live[None], scores, masked_low)
    new_max = jnp.maximum(run_max, jnp.max(scores, axis=2))
    shifted = jnp.where(live[None], jnp.exp(scores - new_max[:, :, None]), 0.0)
    fading = jnp.exp(run_max - new_max)
    new_sum = run_sum * fading + jnp.sum(shifted, axis=2)
    product = jnp.einsum(
        "hqk,khd->qhd", shifted.astype(jnp.bfloat16), value_part, preferred_element_type=jnp.float32
    )
    return (accum * fading.T[:, :, None] + product, new_max, new_sum)


def backward_tile(saved, key_part, value_part, live, score_scale):
    query_heads, grad_heads, log_total, delta = saved
    scores = (
        jnp.einsum("qhd,khd->hqk", query_heads, key_part, preferred_element_type=jnp.float32)
        * score_scale
    )
    probs = jnp.where(live[None], jnp.exp(scores - log_total[:, :, None]), 0.0)
    back_weights = probs.astype(jnp.bfloat16)
    grad_value = jnp.einsum(
        "hqk,qhd->khd", back_weights, grad_heads, preferred_element_type=jnp.float32
    )
    grad_weights = jnp.einsum(
        "qhd,khd->hqk", grad_heads, value_part, preferred_element_type=jnp.float32
    )
    grad_scores = (probs * (grad_weights - delta[:, :, None])).astype(jnp.bfloat16)
    grad_query = (
        jnp.einsum("hqk,khd->qhd", grad_scores, key_part, preferred_element_type=jnp.float32)
        * score_scale
    )
    grad_key = (
        jnp.einsum("hqk,qhd->khd", grad_scores, query_heads, preferred_element_type=jnp.float32)
        * score_scale
    )
    return (grad_query, grad_key, grad_value)


def per_device(queries, keys, values, grad_out, block_doc):
    query_here, key_here, value_here, grad_here = (
        lax.all_to_all(queries, "head", split_axis=1, concat_axis=0, tiled=True),
        lax.all_to_all(keys, "head", split_axis=1, concat_axis=0, tiled=True),
        lax.all_to_all(values, "head", split_axis=1, concat_axis=0, tiled=True),
        lax.all_to_all(grad_out, "head", split_axis=1, concat_axis=0, tiled=True),
    )
    row_count = query_here.shape[0]
    feature_width = query_here.shape[1]
    local_heads = feature_width // HD
    score_scale = HD ** (-0.5)
    cycle_size = lax.axis_size("ctx")
    position = lax.axis_index("ctx")
    query_pos = token_positions(position * row_count, row_count, row_count, cycle_size)
    query_heads = query_here.reshape(row_count, local_heads, HD)
    grad_heads = grad_here.reshape(row_count, local_heads, HD)

    def fold_keys(running, pieces, first_row):
        key_part = pieces[0].reshape(-1, local_heads, HD)
        value_part = pieces[1].reshape(-1, local_heads, HD)
        key_pos = token_positions(first_row, key_part.shape[0], row_count, cycle_size)
        live = visible(block_doc, query_pos, key_pos)
        return forward_update(running, query_heads, key_part, value_part, live, score_scale)

    start_fold = (
        jnp.zeros((row_count, local_heads, HD), jnp.float32),
        jnp.full((local_heads, row_count), masked_low, jnp.float32),
        jnp.zeros((local_heads, row_count), jnp.float32),
    )
    gathered = lax.all_gather(jnp.stack((key_here, value_here)), "ctx", axis=1, tiled=True)
    span = row_count * math.gcd(cycle_size, max(1, 512 // row_count))
    block_total = cycle_size * row_count // span

    def forward_block(block_index, running):
        first_row = block_index * span
        part = lax.dynamic_slice_in_dim(gathered, first_row, span, 1)
        return fold_keys(running, (part[0], part[1]), first_row)

    accum, run_max, run_sum = lax.fori_loop(0, block_total, forward_block, start_fold)
    out_heads = (accum / run_sum.T[:, :, None]).astype(jnp.bfloat16)
    log_total = run_max + jnp.log(run_sum)
    delta = jnp.sum(grad_heads.astype(jnp.float32) * out_heads.astype(jnp.float32), axis=2).T
    saved = (query_heads, grad_heads, log_total, delta)

    def tile_grads(key_flat, value_flat, key_start):
        key_part = key_flat.reshape(-1, local_heads, HD)
        value_part = value_flat.reshape(-1, local_heads, HD)
        key_pos = token_positions(key_start, key_part.shape[0], row_count, cycle_size)
        live = visible(block_doc, query_pos, key_pos)
        return backward_tile(saved, key_part, value_part, live, score_scale)

    def backward_block(block_index, state):
        grad_query, key_sums = state
        first_row = block_index * span
        part = lax.dynamic_slice_in_dim(gathered, first_row, span, 1)
        add_query, add_key, add_value = tile_grads(part[0], part[1], first_row)
        key_sums = lax.dynamic_update_slice_in_dim(
            key_sums, jnp.stack((add_key, add_value)), first_row, 1
        )
        return (grad_query + add_query, key_sums)

    start_back = (
        jnp.zeros((row_count, local_heads, HD), jnp.float32),
        jnp.zeros((2, cycle_size * row_count, local_heads, HD), jnp.float32),
    )
    grad_query, key_sums = lax.fori_loop(0, block_total, backward_block, start_back)
    grad_key, grad_value = (
        lax.psum_scatter(
            key_sums[0].astype(jnp.bfloat16), "ctx", scatter_dimension=0, tiled=True
        ).astype(jnp.float32),
        lax.psum_scatter(
            key_sums[1].astype(jnp.bfloat16), "ctx", scatter_dimension=0, tiled=True
        ).astype(jnp.float32),
    )
    out_flat = out_heads.reshape(row_count, feature_width)
    query_flat = grad_query.astype(jnp.bfloat16).reshape(row_count, feature_width)
    key_flat = grad_key.astype(jnp.bfloat16).reshape(row_count, feature_width)
    value_flat = grad_value.astype(jnp.bfloat16).reshape(row_count, feature_width)
    return (
        lax.all_to_all(out_flat, "head", split_axis=0, concat_axis=1, tiled=True),
        lax.all_to_all(query_flat, "head", split_axis=0, concat_axis=1, tiled=True),
        lax.all_to_all(key_flat, "head", split_axis=0, concat_axis=1, tiled=True),
        lax.all_to_all(value_flat, "head", split_axis=0, concat_axis=1, tiled=True),
    )


def solution(mesh):
    return jax.shard_map(
        per_device,
        mesh=mesh,
        in_specs=(
            P(("ctx", "head"), None),
            P(("ctx", "head"), None),
            P(("ctx", "head"), None),
            P(("ctx", "head"), None),
            P(),
        ),
        out_specs=(
            P(("ctx", "head"), None),
            P(("ctx", "head"), None),
            P(("ctx", "head"), None),
            P(("ctx", "head"), None),
        ),
        check_vma=False,
    )
```

profile of v0, /device:TPU:0, one launch (start us, length us, event | category | flops | bytes accessed | tf_op | source)
XLA Modules:
  0.0 350.0 jit_solution(4947090339236871843)
XLA Ops:
  7.2 1.7 copy.146
  8.9 7.2 %all-to-all-start = ((bf16[32,8,512]{2,0,1:T(8,128)(2,1)}), bf16[32,8,512]{2,0,1:T(8,128)(2,1)S(1)}, u32[]{:S(2)}, u32[]{:S(2)}) async-start(bf16[32,8,512]{2,0,1:T(8,128)(2,1)} %bitcast.94), calls=%async_computation | async-start | bytes 524288 | tf_op jit(solution)/shard_map/all_to_all | solution.py:80
  17.1 7.7 %all-to-all-done = bf16[32,8,512]{2,0,1:T(8,128)(2,1)S(1)} async-done(((bf16[32,8,512]{2,0,1:T(8,128)(2,1)}), bf16[32,8,512]{2,0,1:T(8,128)(2,1)S(1)}, u32[]{:S(2)}, u32[]{:S(2)}) %all-to-all-start) | async-done | bytes 262176 | tf_op jit(solution)/shard_map/all_to_all | solution.py:80
  24.8 11.3 %all_to_all.140 = bf16[32,8,512]{2,0,1:T(8,128)(2,1)S(1)} all-to-all(bf16[32,8,512]{2,0,1:T(8,128)(2,1)S(1)} %bitcast.162), channel_id=1, replica_groups=mesh['ctx'=16,'head'=8] {'head'}, dimensions={1} | all-to-all | bytes 524288 | tf_op jit(solution)/shard_map/all_to_all | solution.py:81
  37.7 3.4 all-to-all-start.2
  41.9 7.9 %all-to-all-done.2 = bf16[32,8,512]{2,0,1:T(8,128)(2,1)S(1)} async-done(((bf16[32,8,512]{2,0,1:T(8,128)(2,1)}), bf16[32,8,512]{2,0,1:T(8,128)(2,1)S(1)}, u32[]{:S(2)}, u32[]{:S(2)}) %all-to-all-start.2) | async-done | bytes 262176 | tf_op jit(solution)/shard_map/all_to_all | solution.py:79
  49.8 3.4 all-to-all-start.4
  53.4 10.4 %all-to-all-done.4 = bf16[32,8,512]{2,0,1:T(8,128)(2,1)S(1)} async-done(((bf16[32,8,512]{2,0,1:T(8,128)(2,1)}), bf16[32,8,512]{2,0,1:T(8,128)(2,1)S(1)}, u32[]{:S(2)}, u32[]{:S(2)}) %all-to-all-start.4) | async-done | bytes 262176 | tf_op jit(solution)/shard_map/all_to_all | solution.py:82
  63.9 26.2 %all-gather.2.cloned.1.call-done = bf16[2,4096,512]{2,1,0:T(8,128)(2,1)} async-done(((bf16[2,256,512]{2,1,0:T(8,128)(2,1)}), bf16[2,4096,512]{2,1,0:T(8,128)(2,1)}) %all-gather.2.cloned.1.call-update) | async-done | bytes 8388624 | tf_op jit(solution)/shard_map/all_gather | solution.py:106
  90.1 11.3 %copy.110 = bf16[2,4096,512]{1,2,0:T(8,128)(2,1)} copy(bf16[2,4096,512]{2,1,0:T(8,128)(2,1)} %all-gather.2.cloned.1.call-done) | data formatting | bytes 16777216
  101.5 29.7 %while.44 = (s32[]{:T(128)}, f32[256,4,128]{0,2,1:T(8,128)S(1)}, f32[4,256]{1,0:T(4,128)S(1)}, f32[4,256]{1,0:T(4,128)S(1)}, s32[32]{0:T(128)S(1)}, /*index=5*/b...) while((s32[]{:T(128)}, f32[256,4,128]{0,2,1:T(8,128)S(1)}, ...), condition=%wide.region_5.6_spmd.clone.clone.clone, body=%wide.region_0.5_spmd.clone.clone.clone.sunk | while | flops 276164096 | bytes 11359203 | solution.py:115
  132.3 4.3 %broadcast_in_dim.271 = bf16[2,4096,4,128]{3,1,2,0:T(8,128)(2,1)} broadcast(bf16[]{:T(256)} %constant.563), dimensions={} | broadcast | bytes 8388610 | tf_op jit(solution)/shard_map/broadcast_in_dim | solution.py:140
  136.6 43.1 %while.45 = (s32[]{:T(128)}, f32[256,4,128]{0,2,1:T(8,128)S(1)}, bf16[2,4096,4,128]{3,1,2,0:T(8,128)(2,1)}, bf16[2,4096,512]{1,2,0:T(8,128)(2,1)}, s32[32]{0:T(1...) while((s32[]{:T(128)}, f32[256,4,128]{0,2,1:T(8,128)S(1)}, ...), condition=%wide.region_10.11_spmd.clone.clone.clone, body=%wide.region_7.10_spmd.clone.clone.clone.sunk | while | flops 678286848 | bytes 18641908 | solution.py:142
  147.8 1.3 constant_dynamic-slice_fusion.7
  153.2 1.3 constant_dynamic-slice_fusion.7
  179.7 5.7 %slice_bitcast_fusion = (bf16[4096,4,128]{2,0,1:T(8,128)(2,1)}, bf16[4096,4,128]{2,0,1:T(8,128)(2,1)}) fusion(bf16[2,4096,4,128]{3,1,2,0:T(8,128)(2,1)} %get-tuple-element.567), kind=kLoop, calls=%fused_computation.121 | loop fusion | bytes 16777216 | tf_op jit(solution)/shard_map/convert_element_type | solution.py:148
  187.0 6.4 %all-to-all-start.3 = ((bf16[8,32,512]{2,1,0:T(8,128)(2,1)}), bf16[8,32,512]{2,1,0:T(8,128)(2,1)S(1)}, u32[]{:S(2)}, u32[]{:S(2)}) async-start(bf16[8,32,512]{2,1,0:T(8,128)(2,1)} %all_to_all.113), calls=%async_computation.3 | async-start | bytes 524288 | tf_op jit(solution)/shard_map/all_to_all | solution.py:156
  194.4 8.1 %all-to-all-done.3 = bf16[8,32,512]{2,1,0:T(8,128)(2,1)S(1)} async-done(((bf16[8,32,512]{2,1,0:T(8,128)(2,1)}), bf16[8,32,512]{2,1,0:T(8,128)(2,1)S(1)}, u32[]{:S(2)}, u32[]{:S(2)}) %all-to-all-start.3) | async-done | bytes 262176 | tf_op jit(solution)/shard_map/all_to_all | solution.py:156
  202.5 3.4 all-to-all-start.5
  205.9 50.0 %reduce-scatter.3.cloned.1.call-done = bf16[256,4,128]{2,0,1:T(8,128)(2,1)} async-done(((bf16[4096,4,128]{2,0,1:T(8,128)(2,1)}), bf16[256,4,128]{2,0,1:T(8,128)(2,1)}) %reduce-scatter.3.cloned.1.call-update) | async-done | bytes 262160 | tf_op jit(solution)/shard_map/reduce_scatter | solution.py:144
  257.8 7.6 %all-to-all-start.6 = ((bf16[8,32,512]{2,1,0:T(8,128)(2,1)}), bf16[8,32,512]{2,1,0:T(8,128)(2,1)S(1)}, u32[]{:S(2)}, u32[]{:S(2)}) async-start(bf16[8,32,512]{2,1,0:T(8,128)(2,1)} %all_to_all.124), calls=%async_computation.7 | async-start | bytes 524288 | tf_op jit(solution)/shard_map/all_to_all | solution.py:158
  265.5 60.2 %reduce-scatter.5.cloned.1.call-done = bf16[256,4,128]{2,0,1:T(8,128)(2,1)} async-done(((bf16[4096,4,128]{2,0,1:T(8,128)(2,1)}), bf16[256,4,128]{2,0,1:T(8,128)(2,1)}) %reduce-scatter.5.cloned.1.call-update) | async-done | bytes 262160 | tf_op jit(solution)/shard_map/reduce_scatter | solution.py:147
  327.6 6.4 %all-to-all-start.7 = ((bf16[8,32,512]{2,1,0:T(8,128)(2,1)}), bf16[8,32,512]{2,1,0:T(8,128)(2,1)S(1)}, u32[]{:S(2)}, u32[]{:S(2)}) async-start(bf16[8,32,512]{2,1,0:T(8,128)(2,1)} %all_to_all.128), calls=%async_computation.9 | async-start | bytes 524288 | tf_op jit(solution)/shard_map/all_to_all | solution.py:159
  336.2 6.6 %all-to-all-done.7 = bf16[8,32,512]{2,1,0:T(8,128)(2,1)S(1)} async-done(((bf16[8,32,512]{2,1,0:T(8,128)(2,1)}), bf16[8,32,512]{2,1,0:T(8,128)(2,1)S(1)}, u32[]{:S(2)}, u32[]{:S(2)}) %all-to-all-start.7) | async-done | bytes 262176 | tf_op jit(solution)/shard_map/all_to_all | solution.py:159
  (265 shorter events, 83.3 us)
Async XLA Ops:
  7.2 29.8 %copy-start = (bf16[32,4096]{1,0:T(8,128)(2,1)S(1)}, bf16[32,4096]{1,0:T(8,128)(2,1)}, u32[]{:S(2)}) copy-start(bf16[32,4096]{1,0:T(8,128)(2,1)} %param.9) | copy-start | bytes 786436
  8.9 32.2 %copy-start.1 = (bf16[32,4096]{1,0:T(8,128)(2,1)S(1)}, bf16[32,4096]{1,0:T(8,128)(2,1)}, u32[]{:S(2)}) copy-start(bf16[32,4096]{1,0:T(8,128)(2,1)} %param.12) | copy-start | bytes 786436
  8.9 15.9 %all-to-all-start = ((bf16[32,8,512]{2,0,1:T(8,128)(2,1)}), bf16[32,8,512]{2,0,1:T(8,128)(2,1)S(1)}, u32[]{:S(2)}, u32[]{:S(2)}) async-start(bf16[32,8,512]{2,0,1:T(8,128)(2,1)} %bitcast.94), calls=%async_computation | async-start | bytes 524288 | tf_op jit(solution)/shard_map/all_to_all | solution.py:80
  16.1 74.0 %all-gather.2.cloned.1.call-start = ((), (), s32[]{:S(2)}) async-start(), calls=%async_computation.10 | async-start | bytes 8912896 | tf_op jit(solution)/shard_map/all_gather | solution.py:106
  37.7 12.1 %all-to-all-start.2 = ((bf16[32,8,512]{2,0,1:T(8,128)(2,1)}), bf16[32,8,512]{2,0,1:T(8,128)(2,1)S(1)}, u32[]{:S(2)}, u32[]{:S(2)}) async-start(bf16[32,8,512]{2,0,1:T(8,128)(2,1)} %bitcast.92), calls=%async_computation.2 | async-start | bytes 524288 | tf_op jit(solution)/shard_map/all_to_all | solution.py:79
  49.8 14.0 %all-to-all-start.4 = ((bf16[32,8,512]{2,0,1:T(8,128)(2,1)}), bf16[32,8,512]{2,0,1:T(8,128)(2,1)S(1)}, u32[]{:S(2)}, u32[]{:S(2)}) async-start(bf16[32,8,512]{2,0,1:T(8,128)(2,1)} %bitcast.91), calls=%async_computation.4 | async-start | bytes 524288 | tf_op jit(solution)/shard_map/all_to_all | solution.py:82
  53.2 202.7 %reduce-scatter.3.cloned.1.call-start = ((), (), s32[]{:S(2)}) async-start(), calls=%async_computation.11 | async-start | bytes 4456448 | tf_op jit(solution)/shard_map/reduce_scatter | solution.py:144
  63.9 37.5 %copy-start.2 = (s32[32]{0:T(128)S(1)}, s32[32]{0:T(128)}, u32[]{:S(2)}) copy-start(s32[32]{0:T(128)} %param.13) | copy-start | bytes 388
  185.4 140.2 %reduce-scatter.5.cloned.1.call-start = ((), (), s32[]{:S(2)}) async-start(), calls=%async_computation.12 | async-start | bytes 4456448 | tf_op jit(solution)/shard_map/reduce_scatter | solution.py:147
  187.0 15.5 %all-to-all-start.3 = ((bf16[8,32,512]{2,1,0:T(8,128)(2,1)}), bf16[8,32,512]{2,1,0:T(8,128)(2,1)S(1)}, u32[]{:S(2)}, u32[]{:S(2)}) async-start(bf16[8,32,512]{2,1,0:T(8,128)(2,1)} %all_to_all.113), calls=%async_computation.3 | async-start | bytes 524288 | tf_op jit(solution)/shard_map/all_to_all | solution.py:156
  202.5 55.3 %all-to-all-start.5 = ((bf16[8,32,512]{2,1,0:T(8,128)(2,1)}), bf16[8,32,512]{2,1,0:T(8,128)(2,1)S(1)}, u32[]{:S(2)}, u32[]{:S(2)}) async-start(bf16[8,32,512]{2,1,0:T(8,128)(2,1)} %all_to_all.120), calls=%async_computation.5 | async-start | bytes 524288 | tf_op jit(solution)/shard_map/all_to_all | solution.py:157
  257.8 69.8 %all-to-all-start.6 = ((bf16[8,32,512]{2,1,0:T(8,128)(2,1)}), bf16[8,32,512]{2,1,0:T(8,128)(2,1)S(1)}, u32[]{:S(2)}, u32[]{:S(2)}) async-start(bf16[8,32,512]{2,1,0:T(8,128)(2,1)} %all_to_all.124), calls=%async_computation.7 | async-start | bytes 524288 | tf_op jit(solution)/shard_map/all_to_all | solution.py:158
  327.6 15.1 %all-to-all-start.7 = ((bf16[8,32,512]{2,1,0:T(8,128)(2,1)}), bf16[8,32,512]{2,1,0:T(8,128)(2,1)S(1)}, u32[]{:S(2)}, u32[]{:S(2)}) async-start(bf16[8,32,512]{2,1,0:T(8,128)(2,1)} %all_to_all.128), calls=%async_computation.9 | async-start | bytes 524288 | tf_op jit(solution)/shard_map/all_to_all | solution.py:159
Sparse Core Ops, SparseCore 0:
  37.1 52.9 all-gather.1
  185.6 70.2 reduce-scatter.2
  258.3 67.2 reduce-scatter.4
where the time goes:
time: 352 us; the launch traced here: 350 us
  waiting for transfers between devices  178 us (51%)
  local copies, waits for them, and re-layouts  55.3 us (16%)
  starting transfers between devices  38 us (11%)
  matrix products  29.8 us (8%)
  other arithmetic  23 us (7%)
  between operations  13.9 us (4%)
  blocking collectives  11.3 us (3%)
    reduce_scatter x1, waiting for transfers between devices, per_device(): lax.psum_scatter(key_sums[1].astype(jnp.bfloat16), 'ctx', scatter_dimensi...  60.2 us
    reduce_scatter x1, waiting for transfers between devices, per_device(): lax.psum_scatter(key_sums[0].astype(jnp.bfloat16), 'ctx', scatter_dimensi...  50 us
    all_gather x1, waiting for transfers between devices, per_device(): lax.all_gather(jnp.stack((key_here, value_here)), 'ctx', axis=1, tiled=True)  26.2 us
    unnamed x10, local copies, waits for them, and re-layouts  11.5 us
    all_to_all x1, blocking collectives, per_device(): lax.all_to_all(values, 'head', split_axis=1, concat_axis=0, tiled=True)  11.3 us
    all_to_all x1, waiting for transfers between devices, per_device(): lax.all_to_all(grad_out, 'head', split_axis=1, concat_axis=0, tiled=True)  10.4 us
    slice x8, local copies, waits for them, and re-layouts, backward_block(): add_query, add_key, add_value = tile_grads(part[0], part[1], first_row)  10.2 us
    slice x8, local copies, waits for them, and re-layouts, forward_block(): return fold_keys(running, (part[0], part[1]), first_row)  10.2 us
  transfers between devices with their start and end apart: 10, of which 8 were waited for; matrix products, arithmetic and copies ran while one was open for 2% of the time, Pallas kernels for 0%

commit v1 on v0

--- a/solution.py
+++ b/solution.py
@@ -3,6 +3,7 @@
 import jax.numpy as jnp
 from jax import lax
 from jax.sharding import PartitionSpec as P
+from jax.lax import all_to_all, axis_size
 
 HD = 128
 BLK = 128
@@ -103,7 +104,14 @@
         jnp.full((local_heads, row_count), masked_low, jnp.float32),
         jnp.zeros((local_heads, row_count), jnp.float32),
     )
-    gathered = lax.all_gather(jnp.stack((key_here, value_here)), "ctx", axis=1, tiled=True)
+
+    def replace_groups_on_mesh(view, axis_no):
+        outcome_arr = axis_size("ctx")
+        response = jnp.stack(outcome_arr * [view], axis=0)
+        answer = all_to_all(response, split_axis=0, axis_name="ctx", concat_axis=0)
+        return jnp.concatenate(answer, axis=axis_no)
+
+    gathered = replace_groups_on_mesh(jnp.stack((key_here, value_here)), 1)
     span = row_count * math.gcd(cycle_size, max(1, 512 // row_count))
     block_total = cycle_size * row_count // span
 

time: 352 us -> 469 us (1.33)
  waiting for transfers between devices: 178 us -> 285 us
  local copies, waits for them, and re-layouts: 55.3 us -> 72.4 us
  blocking collectives: 11.3 us -> 0 us
    all_to_all x0 -> x2, waiting for transfers between devices: none -> 131 us  [the longest x1 123 us: replace_groups_on_mesh(): answer = all_to_all(response, split_axis=0, axis_name='ctx', concat_axis=0)]
    all_gather x1 -> x0, waiting for transfers between devices: 26.2 us -> none  [per_device(): lax.all_gather(jnp.stack((key_here, value_here)), 'ctx', axis=1, tiled=True)]
    all_to_all x0 -> x1, local copies, waits for them, and re-layouts: none -> 11.9 us  [replace_groups_on_mesh(): answer = all_to_all(response, split_axis=0, axis_name='ctx', concat_axis=0)]
    all_to_all x1 -> x0, blocking collectives: 11.3 us -> none  [per_device(): lax.all_to_all(values, 'head', split_axis=1, concat_axis=0, tiled=True)]
    all_to_all x0 -> x2, starting transfers between devices: none -> 8.91 us  [the longest x1 5.5 us: replace_groups_on_mesh(): answer = all_to_all(response, split_axis=0, axis_name='ctx', concat_axis=0)]
    reduce_scatter x1, waiting for transfers between devices: 50 us -> 55.9 us  [per_device(): lax.psum_scatter(key_sums[0].astype(jnp.bfloat16), 'ctx', scatter_dimensi...]
  transfers between devices with their start and end apart: 10 -> 11, of which waited for: 8 -> 9; matrix products, arithmetic and copies ran while one was open for 2% -> 2% of each run, Pallas kernels for 0% -> 0%
where the time goes in v1:
time: 469 us; the launch traced here: 467 us
  waiting for transfers between devices  285 us (61%)
  local copies, waits for them, and re-layouts  72.4 us (15%)
  starting transfers between devices  42 us (9%)
  matrix products  29.8 us (6%)
  other arithmetic  22.4 us (5%)
  between operations  14.3 us (3%)
    all_to_all x1, waiting for transfers between devices, replace_groups_on_mesh(): answer = all_to_all(response, split_axis=0, axis_name='ctx', concat_axis=0)  123 us
    reduce_scatter x1, waiting for transfers between devices, per_device(): lax.psum_scatter(key_sums[1].astype(jnp.bfloat16), 'ctx', scatter_dimensi...  60 us
    reduce_scatter x1, waiting for transfers between devices, per_device(): lax.psum_scatter(key_sums[0].astype(jnp.bfloat16), 'ctx', scatter_dimensi...  55.9 us
    all_to_all x1, local copies, waits for them, and re-layouts, replace_groups_on_mesh(): answer = all_to_all(response, split_axis=0, axis_name='ctx', concat_axis=0)  11.9 us
    unnamed x10, local copies, waits for them, and re-layouts  11.6 us
    slice x8, local copies, waits for them, and re-layouts, backward_block(): add_query, add_key, add_value = tile_grads(part[0], part[1], first_row)  10.2 us
    slice x8, local copies, waits for them, and re-layouts, forward_block(): return fold_keys(running, (part[0], part[1]), first_row)  10.2 us
    dynamic_update_slice x8, other arithmetic, backward_block(): lax.dynamic_update_slice_in_dim(key_sums, jnp.stack((add_key, add_value))...  9.38 us
  transfers between devices with their start and end apart: 11, of which 9 were waited for; matrix products, arithmetic and copies ran while one was open for 2% of the time, Pallas kernels for 0%

profile of v1, /device:TPU:0, one launch (start us, length us, event | category | flops | bytes accessed | tf_op | source)
XLA Modules:
  0.0 467.0 jit_solution(15217793196948300683)
XLA Ops:
  8.9 7.0 %all-to-all-start.3 = ((bf16[32,8,512]{2,0,1:T(8,128)(2,1)}), bf16[32,8,512]{2,0,1:T(8,128)(2,1)S(1)}, u32[]{:S(2)}, u32[]{:S(2)}) async-start(bf16[32,8,512]{2,0,1:T(8,128)(2,1)} %bitcast.95), calls=%async_computation.3 | async-start | bytes 524288 | tf_op jit(solution)/shard_map/all_to_all | solution.py:80
  17.6 7.1 %all-to-all-done.3 = bf16[32,8,512]{2,0,1:T(8,128)(2,1)S(1)} async-done(((bf16[32,8,512]{2,0,1:T(8,128)(2,1)}), bf16[32,8,512]{2,0,1:T(8,128)(2,1)S(1)}, u32[]{:S(2)}, u32[]{:S(2)}) %all-to-all-start.3) | async-done | bytes 262176 | tf_op jit(solution)/shard_map/all_to_all | solution.py:80
  24.7 3.4 all-to-all-start
  28.8 7.9 %all-to-all-done = bf16[32,8,512]{2,0,1:T(8,128)(2,1)S(1)} async-done(((bf16[32,8,512]{2,0,1:T(8,128)(2,1)}), bf16[32,8,512]{2,0,1:T(8,128)(2,1)S(1)}, u32[]{:S(2)}, u32[]{:S(2)}) %all-to-all-start) | async-done | bytes 262176 | tf_op jit(solution)/shard_map/all_to_all | solution.py:81
  36.8 3.4 all-to-all-start.1
  40.9 7.9 %all-to-all-done.1 = bf16[32,8,512]{2,0,1:T(8,128)(2,1)S(1)} async-done(((bf16[32,8,512]{2,0,1:T(8,128)(2,1)}), bf16[32,8,512]{2,0,1:T(8,128)(2,1)S(1)}, u32[]{:S(2)}, u32[]{:S(2)}) %all-to-all-start.1) | async-done | bytes 262176 | tf_op jit(solution)/shard_map/all_to_all | solution.py:82
  48.9 3.4 all-to-all-start.5
  52.5 8.4 %all-to-all-done.5 = bf16[32,8,512]{2,0,1:T(8,128)(2,1)S(1)} async-done(((bf16[32,8,512]{2,0,1:T(8,128)(2,1)}), bf16[32,8,512]{2,0,1:T(8,128)(2,1)S(1)}, u32[]{:S(2)}, u32[]{:S(2)}) %all-to-all-start.5) | async-done | bytes 262176 | tf_op jit(solution)/shard_map/all_to_all | solution.py:83
  60.9 4.2 stack.64
  65.1 5.5 %all-to-all-start.2 = ((bf16[16,2,256,512]{2,3,1,0:T(8,128)(2,1)}), bf16[16,2,256,512]{2,3,1,0:T(8,128)(2,1)}, u32[]{:S(2)}, u32[]{:S(2)}) async-start(bf16[16,2,256,512]{2,3,1,0:T(8,128)(2,1)} %stack.64), calls=%async_computation.2 | async-start | bytes 16777216 | tf_op jit(solution)/shard_map/all_to_all | solution.py:111
  70.9 123.0 %all-to-all-done.2 = bf16[16,2,256,512]{2,3,1,0:T(8,128)(2,1)} async-done(((bf16[16,2,256,512]{2,3,1,0:T(8,128)(2,1)}), bf16[16,2,256,512]{2,3,1,0:T(8,128)(2,1)}, u32[]{:S(2)}, u32[]{:S(2)}) %all-to-all-start.2) | async-done | bytes 8388640 | tf_op jit(solution)/shard_map/all_to_all | solution.py:111
  193.9 11.9 %copy.110 = bf16[16,2,256,512]{3,2,0,1:T(8,128)(2,1)} copy(bf16[16,2,256,512]{2,3,1,0:T(8,128)(2,1)} %all-to-all-done.2) | data formatting | bytes 16777216 | tf_op jit(solution)/shard_map/all_to_all | solution.py:111
  205.8 11.4 %copy.112 = bf16[2,4096,512]{1,2,0:T(8,128)(2,1)} copy(bf16[2,4096,512]{2,1,0:T(8,128)(2,1)} %bitcast.158) | data formatting | bytes 16777216
  217.3 29.7 %while.44 = (s32[]{:T(128)}, f32[256,4,128]{0,2,1:T(8,128)S(1)}, f32[4,256]{1,0:T(4,128)S(1)}, f32[4,256]{1,0:T(4,128)S(1)}, s32[32]{0:T(128)S(1)}, /*index=5*/b...) while((s32[]{:T(128)}, f32[256,4,128]{0,2,1:T(8,128)S(1)}, ...), condition=%wide.region_5.6_spmd.clone.clone.clone, body=%wide.region_0.5_spmd.clone.clone.clone.sunk | while | flops 276164096 | bytes 11359203 | solution.py:123
  248.1 4.3 broadcast_in_dim.271
  252.4 43.3 %while.45 = (s32[]{:T(128)}, f32[256,4,128]{0,2,1:T(8,128)S(1)}, bf16[2,4096,4,128]{3,1,2,0:T(8,128)(2,1)}, bf16[2,4096,512]{1,2,0:T(8,128)(2,1)}, s32[32]{0:T(1...) while((s32[]{:T(128)}, f32[256,4,128]{0,2,1:T(8,128)S(1)}, ...), condition=%wide.region_10.11_spmd.clone.clone.clone, body=%wide.region_7.10_spmd.clone.clone.clone.sunk | while | flops 678286848 | bytes 18641908 | solution.py:150
  295.7 5.7 %slice_bitcast_fusion = (bf16[4096,4,128]{2,0,1:T(8,128)(2,1)}, bf16[4096,4,128]{2,0,1:T(8,128)(2,1)}) fusion(bf16[2,4096,4,128]{3,1,2,0:T(8,128)(2,1)} %get-tuple-element.567), kind=kLoop, calls=%fused_computation.121 | loop fusion | bytes 16777216 | tf_op jit(solution)/shard_map/convert_element_type | solution.py:156
  307.5 7.7 %all-to-all-done.4 = bf16[8,32,512]{2,1,0:T(8,128)(2,1)S(1)} async-done(((bf16[8,32,512]{2,1,0:T(8,128)(2,1)}), bf16[8,32,512]{2,1,0:T(8,128)(2,1)S(1)}, u32[]{:S(2)}, u32[]{:S(2)}) %all-to-all-start.4) | async-done | bytes 262176 | tf_op jit(solution)/shard_map/all_to_all | solution.py:164
  315.2 3.4 all-to-all-start.6
  318.6 55.9 %reduce-scatter.3.cloned.1.call-done = bf16[256,4,128]{2,0,1:T(8,128)(2,1)} async-done(((bf16[4096,4,128]{2,0,1:T(8,128)(2,1)}), bf16[256,4,128]{2,0,1:T(8,128)(2,1)}) %reduce-scatter.3.cloned.1.call-update) | async-done | bytes 262160 | tf_op jit(solution)/shard_map/reduce_scatter | solution.py:152
  376.5 5.9 %all-to-all-start.7 = ((bf16[8,32,512]{2,1,0:T(8,128)(2,1)}), bf16[8,32,512]{2,1,0:T(8,128)(2,1)S(1)}, u32[]{:S(2)}, u32[]{:S(2)}) async-start(bf16[8,32,512]{2,1,0:T(8,128)(2,1)} %all_to_all.128), calls=%async_computation.8 | async-start | bytes 524288 | tf_op jit(solution)/shard_map/all_to_all | solution.py:166
  382.4 60.0 %reduce-scatter.5.cloned.1.call-done = bf16[256,4,128]{2,0,1:T(8,128)(2,1)} async-done(((bf16[4096,4,128]{2,0,1:T(8,128)(2,1)}), bf16[256,4,128]{2,0,1:T(8,128)(2,1)}) %reduce-scatter.5.cloned.1.call-update) | async-done | bytes 262160 | tf_op jit(solution)/shard_map/reduce_scatter | solution.py:155
  444.3 6.4 %all-to-all-start.8 = ((bf16[8,32,512]{2,1,0:T(8,128)(2,1)}), bf16[8,32,512]{2,1,0:T(8,128)(2,1)S(1)}, u32[]{:S(2)}, u32[]{:S(2)}) async-start(bf16[8,32,512]{2,1,0:T(8,128)(2,1)} %all_to_all.132), calls=%async_computation.10 | async-start | bytes 524288 | tf_op jit(solution)/shard_map/all_to_all | solution.py:167
  452.9 6.6 %all-to-all-done.8 = bf16[8,32,512]{2,1,0:T(8,128)(2,1)S(1)} async-done(((bf16[8,32,512]{2,1,0:T(8,128)(2,1)}), bf16[8,32,512]{2,1,0:T(8,128)(2,1)S(1)}, u32[]{:S(2)}, u32[]{:S(2)}) %all-to-all-start.8) | async-done | bytes 262176 | tf_op jit(solution)/shard_map/all_to_all | solution.py:167
  (268 shorter events, 91.3 us)
Async XLA Ops:
  7.2 20.9 %copy-start = (bf16[32,4096]{1,0:T(8,128)(2,1)S(1)}, bf16[32,4096]{1,0:T(8,128)(2,1)}, u32[]{:S(2)}) copy-start(bf16[32,4096]{1,0:T(8,128)(2,1)} %param.11) | copy-start | bytes 786436
  7.2 33.0 %copy-start.1 = (bf16[32,4096]{1,0:T(8,128)(2,1)S(1)}, bf16[32,4096]{1,0:T(8,128)(2,1)}, u32[]{:S(2)}) copy-start(bf16[32,4096]{1,0:T(8,128)(2,1)} %param.12) | copy-start | bytes 786436
  8.9 15.8 %all-to-all-start.3 = ((bf16[32,8,512]{2,0,1:T(8,128)(2,1)}), bf16[32,8,512]{2,0,1:T(8,128)(2,1)S(1)}, u32[]{:S(2)}, u32[]{:S(2)}) async-start(bf16[32,8,512]{2,0,1:T(8,128)(2,1)} %bitcast.95), calls=%async_computation.3 | async-start | bytes 524288 | tf_op jit(solution)/shard_map/all_to_all | solution.py:80
  24.7 12.1 %all-to-all-start = ((bf16[32,8,512]{2,0,1:T(8,128)(2,1)}), bf16[32,8,512]{2,0,1:T(8,128)(2,1)S(1)}, u32[]{:S(2)}, u32[]{:S(2)}) async-start(bf16[32,8,512]{2,0,1:T(8,128)(2,1)} %bitcast.97), calls=%async_computation | async-start | bytes 524288 | tf_op jit(solution)/shard_map/all_to_all | solution.py:81
  36.8 12.1 %all-to-all-start.1 = ((bf16[32,8,512]{2,0,1:T(8,128)(2,1)}), bf16[32,8,512]{2,0,1:T(8,128)(2,1)S(1)}, u32[]{:S(2)}, u32[]{:S(2)}) async-start(bf16[32,8,512]{2,0,1:T(8,128)(2,1)} %bitcast.96), calls=%async_computation.1 | async-start | bytes 524288 | tf_op jit(solution)/shard_map/all_to_all | solution.py:82
  48.9 12.1 %all-to-all-start.5 = ((bf16[32,8,512]{2,0,1:T(8,128)(2,1)}), bf16[32,8,512]{2,0,1:T(8,128)(2,1)S(1)}, u32[]{:S(2)}, u32[]{:S(2)}) async-start(bf16[32,8,512]{2,0,1:T(8,128)(2,1)} %bitcast.94), calls=%async_computation.5 | async-start | bytes 524288 | tf_op jit(solution)/shard_map/all_to_all | solution.py:83
  65.1 128.8 %all-to-all-start.2 = ((bf16[16,2,256,512]{2,3,1,0:T(8,128)(2,1)}), bf16[16,2,256,512]{2,3,1,0:T(8,128)(2,1)}, u32[]{:S(2)}, u32[]{:S(2)}) async-start(bf16[16,2,256,512]{2,3,1,0:T(8,128)(2,1)} %stack.64), calls=%async_computation.2 | async-start | bytes 16777216 | tf_op jit(solution)/shard_map/all_to_all | solution.py:111
  70.6 303.9 %reduce-scatter.3.cloned.1.call-start = ((), (), s32[]{:S(2)}) async-start(), calls=%async_computation.11 | async-start | bytes 4456448 | tf_op jit(solution)/shard_map/reduce_scatter | solution.py:152
  205.8 11.4 %copy-start.2 = (s32[32]{0:T(128)S(1)}, s32[32]{0:T(128)}, u32[]{:S(2)}) copy-start(s32[32]{0:T(128)} %param.13) | copy-start | bytes 388
  301.5 140.9 %reduce-scatter.5.cloned.1.call-start = ((), (), s32[]{:S(2)}) async-start(), calls=%async_computation.12 | async-start | bytes 4456448 | tf_op jit(solution)/shard_map/reduce_scatter | solution.py:155
  303.0 12.2 %all-to-all-start.4 = ((bf16[8,32,512]{2,1,0:T(8,128)(2,1)}), bf16[8,32,512]{2,1,0:T(8,128)(2,1)S(1)}, u32[]{:S(2)}, u32[]{:S(2)}) async-start(bf16[8,32,512]{2,1,0:T(8,128)(2,1)} %all_to_all.117), calls=%async_computation.4 | async-start | bytes 524288 | tf_op jit(solution)/shard_map/all_to_all | solution.py:164
  315.2 61.2 %all-to-all-start.6 = ((bf16[8,32,512]{2,1,0:T(8,128)(2,1)}), bf16[8,32,512]{2,1,0:T(8,128)(2,1)S(1)}, u32[]{:S(2)}, u32[]{:S(2)}) async-start(bf16[8,32,512]{2,1,0:T(8,128)(2,1)} %all_to_all.124), calls=%async_computation.6 | async-start | bytes 524288 | tf_op jit(solution)/shard_map/all_to_all | solution.py:165
  376.5 67.8 %all-to-all-start.7 = ((bf16[8,32,512]{2,1,0:T(8,128)(2,1)}), bf16[8,32,512]{2,1,0:T(8,128)(2,1)S(1)}, u32[]{:S(2)}, u32[]{:S(2)}) async-start(bf16[8,32,512]{2,1,0:T(8,128)(2,1)} %all_to_all.128), calls=%async_computation.8 | async-start | bytes 524288 | tf_op jit(solution)/shard_map/all_to_all | solution.py:166
  444.3 15.1 %all-to-all-start.8 = ((bf16[8,32,512]{2,1,0:T(8,128)(2,1)}), bf16[8,32,512]{2,1,0:T(8,128)(2,1)S(1)}, u32[]{:S(2)}, u32[]{:S(2)}) async-start(bf16[8,32,512]{2,1,0:T(8,128)(2,1)} %all_to_all.132), calls=%async_computation.10 | async-start | bytes 524288 | tf_op jit(solution)/shard_map/all_to_all | solution.py:167
Sparse Core Ops, SparseCore 0:
  301.6 72.8 reduce-scatter.2
  376.9 65.3 reduce-scatter.4
